TPU v7x, 256 devices: a whole 4x4x8 slice. The times are simulated.
256 devices in a mesh: ctx: 64 (over y_lo, x, z), head: 4 (over y_hi, core).
Axes of the slice: x: 4, y: 4 (y_hi: 2, y_lo: 2; y = y_hi * 2 + y_lo), z: 8, core: 2. Of those that a mesh axis runs over, the one named last changes fastest.
Arguments:
- queries: bfloat16 [12288, 768], P(('ctx', 'head')), may hold values from -2.5 to 2.5
- keys: bfloat16 [12288, 768], P(('ctx', 'head')), may hold values from -2.5 to 2.5
- values: bfloat16 [12288, 768], P(('ctx', 'head')), may hold values from -6 to 6
- attended: bfloat16 [12288, 768], P(('ctx', 'head')), may hold values from -6 to 6
- grad_out: bfloat16 [12288, 768], P(('ctx', 'head')), may hold values from -6 to 6
- logsumexp: float32 [12288, 12], P('ctx', 'head'), may hold values from 5 to 8
Outputs:
- grad_queries: bfloat16 [12288, 768], P(('ctx', 'head'))
- grad_keys: bfloat16 [12288, 768], P(('ctx', 'head'))
- grad_values: bfloat16 [12288, 768], P(('ctx', 'head'))
All inputs are finite; a program needn't handle non-finite values.
Results may differ from a plain program's by a relative error of at most 0.0051.
Values may be sent and summed in bfloat16 or wider, within the bound.
A program may use at most 128 MiB of HBM per device.

v0:
```python
import jax
import jax.numpy as jnp
from jax import lax
from jax.sharding import PartitionSpec as P


def block_rows(length):
    for candidate in (2048, 1024, 512):
        return candidate
    return length


def over_blocks(advance, totals, tensors):
    length = tensors[0].shape[0]
    block_size = block_rows(length)
    stacked = tuple(
        (
            matrix.reshape((length // block_size, block_size) + matrix.shape[1:])
            for matrix in tensors
        )
    )

    def single(current, blocks):
        return (advance(current, blocks), None)

    return lax.scan(single, totals, stacked)[0]


def attend(query_part, grad_part, norm_part, delta_part, key_part, value_part, scaling):
    scores = (
        jnp.einsum("ahd,bhd->hab", query_part, key_part, preferred_element_type=jnp.float32)
        * scaling
    )
    weights = jnp.exp(scores - jnp.transpose(norm_part)[:, :, None])
    weights_low = weights.astype(jnp.bfloat16)
    dweights = jnp.einsum("ahd,bhd->hab", grad_part, value_part, preferred_element_type=jnp.float32)
    dscores = (weights * (dweights - jnp.transpose(delta_part)[:, :, None])).astype(jnp.bfloat16)
    return (weights_low, dscores)


def query_term(dscores, key_part, scaling):
    return (
        jnp.einsum("hab,bhd->ahd", dscores, key_part, preferred_element_type=jnp.float32) * scaling
    )


def key_terms(weights_low, dscores, query_part, grad_part, scaling):
    grad_key = (
        jnp.einsum("hab,ahd->bhd", dscores, query_part, preferred_element_type=jnp.float32)
        * scaling
    )
    grad_value = jnp.einsum(
        "hab,ahd->bhd", weights_low, grad_part, preferred_element_type=jnp.float32
    )
    return (grad_key, grad_value)


def local(queries, keys, values, attended, grad_out, logsumexp):
    heads_local = logsumexp.shape[1]
    group_size = lax.axis_size("head")
    width_local = queries.shape[1] // group_size
    head_width = width_local // heads_local
    scaling = head_width ** (-0.5)
    moved = (
        lax.all_to_all(queries, "head", split_axis=1, concat_axis=0, tiled=True),
        lax.all_to_all(keys, "head", split_axis=1, concat_axis=0, tiled=True),
        lax.all_to_all(values, "head", split_axis=1, concat_axis=0, tiled=True),
        lax.all_to_all(grad_out, "head", split_axis=1, concat_axis=0, tiled=True),
        lax.all_to_all(attended, "head", split_axis=1, concat_axis=0, tiled=True),
    )
    length = moved[0].shape[0]

    def split(piece):
        return piece.reshape(piece.shape[0], heads_local, head_width)

    local_q, local_k, local_v, local_g, local_o = [split(matrix) for matrix in moved]
    deltas = jnp.sum(local_g.astype(jnp.float32) * local_o.astype(jnp.float32), axis=2)
    zeros = jnp.zeros((length, heads_local, head_width), jnp.float32)

    def keys_step(grad_query, blocks):
        key_part, value_part = blocks
        dscores = attend(local_q, local_g, logsumexp, deltas, key_part, value_part, scaling)[1]
        return grad_query + query_term(dscores, key_part, scaling)

    def queries_step(totals, blocks):
        query_part, grad_part, norm_part, delta_part = blocks
        weights_low, dscores = attend(
            query_part, grad_part, norm_part, delta_part, local_k, local_v, scaling
        )
        grad_key, grad_value = key_terms(weights_low, dscores, query_part, grad_part, scaling)
        return (totals[0] + grad_key, totals[1] + grad_value)

    all_norms, all_deltas = (
        lax.all_gather(logsumexp, "ctx", axis=0, tiled=True),
        lax.all_gather(deltas, "ctx", axis=0, tiled=True),
    )
    pieces = (
        lax.all_gather(moved[1], "ctx", axis=0, tiled=True),
        lax.all_gather(moved[2], "ctx", axis=0, tiled=True),
    )
    key_piece, value_piece = [split(piece) for piece in pieces]
    grad_query = over_blocks(keys_step, zeros, (key_piece, value_piece))
    pieces = (
        lax.all_gather(moved[0], "ctx", axis=0, tiled=True),
        lax.all_gather(moved[3], "ctx", axis=0, tiled=True),
    )
    query_piece, grad_piece = [split(piece) for piece in pieces]
    grad_key, grad_value = over_blocks(
        queries_step, (zeros, zeros), (query_piece, grad_piece, all_norms, all_deltas)
    )
    query_low = grad_query.reshape(length, width_local).astype(jnp.bfloat16)
    key_low = grad_key.reshape(length, width_local).astype(jnp.bfloat16)
    value_low = grad_value.reshape(length, width_local).astype(jnp.bfloat16)
    grad_queries, grad_keys, grad_values = (
        lax.all_to_all(query_low, "head", split_axis=0, concat_axis=1, tiled=True),
        lax.all_to_all(key_low, "head", split_axis=0, concat_axis=1, tiled=True),
        lax.all_to_all(value_low, "head", split_axis=0, concat_axis=1, tiled=True),
    )
    return (grad_queries, grad_keys, grad_values)


def solution(mesh):
    in_specs = (
        P(("ctx", "head"), None),
        P(("ctx", "head"), None),
        P(("ctx", "head"), None),
        P(("ctx", "head"), None),
        P(("ctx", "head"), None),
        P("ctx", "head"),
    )
    out_specs = (P(("ctx", "head"), None), P(("ctx", "head"), None), P(("ctx", "head"), None))
    return jax.shard_map(local, mesh=mesh, in_specs=in_specs, out_specs=out_specs, check_vma=False)
```

profile of v0, /device:TPU:1, one launch (start us, length us, event | category | flops | bytes accessed | tf_op | source)
XLA Modules:
  0.0 1368.2 jit_solution(7273158289976480809)
XLA Ops:
  7.2 1.0 all_to_all.106
  8.3 11.1 all_to_all.137
  19.5 1.0 all_to_all.113
  20.5 8.9 all_to_all.138
  29.4 1.0 all_to_all.102
  30.5 8.8 all_to_all.139
  39.4 1.0 all_to_all.109
  40.5 10.2 all_to_all.140
  50.7 1.1 all_to_all.116
  52.4 4.9 all-to-all-start.4
  57.3 135.5 %all-gather = f32[64,192,3]{1,2,0:T(4,128)S(1)} all-gather(f32[1,192,3]{1,2,0:T(4,128)} %bitcast.128), channel_id=1, replica_groups=mesh['ctx'=64,'head'=4] {'ctx'}, dimensions={0}, use_global_device_ids=true | all-gather | bytes 149760 | tf_op jit(solution)/shard_map/all_gather | solution.py:94
  192.9 1.0 reshape.70
  194.4 127.4 %all-gather.1 = f32[64,192,3]{1,2,0:T(4,128)S(1)} all-gather(f32[1,192,3]{1,2,0:T(4,128)S(1)} %copy.110), channel_id=1, replica_groups=mesh['ctx'=64,'head'=4] {'ctx'}, dimensions={0}, use_global_device_ids=true | all-gather | bytes 149760 | tf_op jit(solution)/shard_map/all_gather | solution.py:95
  322.6 23.3 %reshape.85 = bf16[6,2048,3,64]{3,2,1,0:T(4,128)(2,1)} reshape(bf16[12288,192]{1,0:T(8,128)(2,1)} %all-gather.11.cloned.1.call-done) | data formatting | bytes 9437184 | tf_op jit(solution)/shard_map/reshape;reshape | solution.py:18
  345.9 17.8 %copy.112 = bf16[6,2048,3,64]{1,3,2,0:T(8,128)(2,1)} copy(bf16[6,2048,3,64]{3,2,1,0:T(4,128)(2,1)} %reshape.85) | data formatting | bytes 9437184
  363.7 231.7 %all-gather.13.cloned.1.call-done = bf16[12288,192]{1,0:T(8,128)(2,1)} async-done(((bf16[192,192]{1,0:T(8,128)(2,1)}), bf16[12288,192]{1,0:T(8,128)(2,1)}) %all-gather.13.cloned.1.call-update) | async-done | bytes 4718608 | tf_op jit(solution)/shard_map/all_gather | solution.py:105
  595.4 23.3 %reshape.86 = bf16[6,2048,3,64]{3,2,1,0:T(4,128)(2,1)} reshape(bf16[12288,192]{1,0:T(8,128)(2,1)} %all-gather.13.cloned.1.call-done) | data formatting | bytes 9437184 | tf_op jit(solution)/shard_map/reshape;reshape | solution.py:18
  618.6 17.8 %copy.115 = bf16[6,2048,3,64]{1,3,2,0:T(8,128)(2,1)} copy(bf16[6,2048,3,64]{3,2,1,0:T(4,128)(2,1)} %reshape.86) | data formatting | bytes 9437184
  636.4 74.3 %while.25 = (s32[]{:T(128)}, f32[192,3,64]{0,2,1:T(8,128)S(1)}, f32[192,3,64]{0,2,1:T(8,128)S(1)}, bf16[6,2048,3,64]{1,3,2,0:T(8,128)(2,1)}, bf16[192,3,64]{0,2,...) while((s32[]{:T(128)}, f32[192,3,64]{0,2,1:T(8,128)S(1)}, ...), condition=%wide.region_4.5_spmd.clone, body=%wide.region_3.4_spmd.clone.sunk | while | flops 613601280 | bytes 18311292 | solution.py:26
  636.4 4.1 fusion.84
  640.6 4.6 fusion.85
  645.2 3.6 fusion.86
  648.8 4.1 fusion.84
  653.0 4.6 fusion.85
  657.6 3.6 fusion.86
  661.2 4.1 fusion.84
  665.4 4.6 fusion.85
  670.0 3.6 fusion.86
  673.6 4.1 fusion.84
  677.8 4.6 fusion.85
  682.3 3.6 fusion.86
  686.0 4.1 fusion.84
  690.1 4.6 fusion.85
  694.7 3.6 fusion.86
  698.4 4.1 fusion.84
  702.5 4.6 fusion.85
  707.1 3.6 fusion.86
  710.9 0.8 copy.131
  711.7 47.2 %all-to-all-start.6 = ((bf16[4,48,192]{2,1,0:T(8,128)(2,1)}), bf16[4,48,192]{2,1,0:T(8,128)(2,1)S(1)}, u32[]{:S(2)}, u32[]{:S(2)}) async-start(bf16[4,48,192]{2,1,0:T(8,128)(2,1)} %copy.131), calls=%async_computation.6 | async-start | bytes 196608 | tf_op jit(solution)/shard_map/all_to_all | solution.py:116
  759.6 0.8 copy.132
  760.4 143.0 %all-gather.7.cloned.1.call-done = bf16[12288,192]{1,0:T(8,128)(2,1)} async-done(((bf16[192,192]{1,0:T(8,128)(2,1)}), bf16[12288,192]{1,0:T(8,128)(2,1)}) %all-gather.7.cloned.1.call-update) | async-done | bytes 4718608 | tf_op jit(solution)/shard_map/all_gather | solution.py:98
  903.4 23.3 %reshape.82 = bf16[6,2048,3,64]{3,2,1,0:T(4,128)(2,1)} reshape(bf16[12288,192]{1,0:T(8,128)(2,1)} %all-gather.7.cloned.1.call-done) | data formatting | bytes 9437184 | tf_op jit(solution)/shard_map/reshape;reshape | solution.py:18
  926.7 17.8 %copy.100 = bf16[6,2048,3,64]{1,3,2,0:T(8,128)(2,1)} copy(bf16[6,2048,3,64]{3,2,1,0:T(4,128)(2,1)} %reshape.82) | data formatting | bytes 9437184
  944.5 266.3 %all-gather.9.cloned.1.call-done = bf16[12288,192]{1,0:T(8,128)(2,1)} async-done(((bf16[192,192]{1,0:T(8,128)(2,1)}), bf16[12288,192]{1,0:T(8,128)(2,1)}) %all-gather.9.cloned.1.call-update) | async-done | bytes 4718608 | tf_op jit(solution)/shard_map/all_gather | solution.py:99
  1210.8 23.3 %reshape.83 = bf16[6,2048,3,64]{3,2,1,0:T(4,128)(2,1)} reshape(bf16[12288,192]{1,0:T(8,128)(2,1)} %all-gather.9.cloned.1.call-done) | data formatting | bytes 9437184 | tf_op jit(solution)/shard_map/reshape;reshape | solution.py:18
  1234.1 17.8 %copy.102 = bf16[6,2048,3,64]{1,3,2,0:T(8,128)(2,1)} copy(bf16[6,2048,3,64]{3,2,1,0:T(4,128)(2,1)} %reshape.83) | data formatting | bytes 9437184
  1251.9 45.7 %all-to-all-start.7 = ((bf16[4,48,192]{2,1,0:T(8,128)(2,1)}), bf16[4,48,192]{2,1,0:T(8,128)(2,1)S(1)}, u32[]{:S(2)}, u32[]{:S(2)}) async-start(bf16[4,48,192]{2,1,0:T(8,128)(2,1)} %copy.132), calls=%async_computation.7 | async-start | bytes 196608 | tf_op jit(solution)/shard_map/all_to_all | solution.py:117
  1297.6 52.6 %while.24 = (s32[]{:T(128)}, f32[192,3,64]{0,2,1:T(8,128)S(1)}, bf16[6,2048,3,64]{1,3,2,0:T(8,128)(2,1)}, bf16[192,3,64]{0,2,1:T(8,128)(2,1)S(1)}, f32[192,3]{0,...) while((s32[]{:T(128)}, f32[192,3,64]{0,2,1:T(8,128)S(1)}, ...), condition=%wide.region_2.3_spmd.clone, body=%wide.region_1.2_spmd.clone.sunk | while | flops 458993664 | bytes 12245103 | solution.py:26
  1297.6 4.1 fusion.75
  1301.7 4.7 fusion.76
  1306.4 4.1 fusion.75
  1310.5 4.7 fusion.76
  1315.1 4.1 fusion.75
  1319.2 4.7 fusion.76
  1323.9 4.1 fusion.75
  1328.0 4.7 fusion.76
  1332.7 4.1 fusion.75
  1336.8 4.7 fusion.76
  1341.4 4.1 fusion.75
  1345.5 4.7 fusion.76
  1350.4 0.8 copy.126
  1351.2 4.8 all-to-all-start.5
  1356.8 0.7 all_to_all.128
  1357.6 3.2 all-to-all-done.5
  (73 shorter events, 5.4 us)
Async XLA Ops:
  7.2 315.4 %all-gather.11.cloned.1.call-start = ((), (), s32[]{:S(2)}) async-start(), calls=%async_computation.10 | async-start | bytes 6389760 | tf_op jit(solution)/shard_map/all_gather | solution.py:104
  19.4 575.9 %all-gather.13.cloned.1.call-start = ((), (), s32[]{:S(2)}) async-start(), calls=%async_computation.11 | async-start | bytes 6389760 | tf_op jit(solution)/shard_map/all_gather | solution.py:105
  29.4 874.0 %all-gather.7.cloned.1.call-start = ((), (), s32[]{:S(2)}) async-start(), calls=%async_computation.8 | async-start | bytes 6389760 | tf_op jit(solution)/shard_map/all_gather | solution.py:98
  39.3 282.7 %copy-start.1 = (bf16[48,4,192]{2,0,1:T(8,128)(2,1)S(1)}, bf16[48,4,192]{2,0,1:T(8,128)(2,1)}, u32[]{:S(2)}) copy-start(bf16[48,4,192]{2,0,1:T(8,128)(2,1)} %all_to_all.139) | copy-start | bytes 221188
  39.4 1171.4 %all-gather.9.cloned.1.call-start = ((), (), s32[]{:S(2)}) async-start(), calls=%async_computation.9 | async-start | bytes 6389760 | tf_op jit(solution)/shard_map/all_gather | solution.py:99
  50.6 271.7 %copy-start.2 = (bf16[48,4,192]{2,0,1:T(8,128)(2,1)S(1)}, bf16[48,4,192]{2,0,1:T(8,128)(2,1)}, u32[]{:S(2)}) copy-start(bf16[48,4,192]{2,0,1:T(8,128)(2,1)} %all_to_all.140) | copy-start | bytes 221188
  52.4 141.5 %all-to-all-start.4 = ((bf16[48,4,192]{2,0,1:T(8,128)(2,1)}), bf16[48,4,192]{2,0,1:T(8,128)(2,1)S(1)}, u32[]{:S(2)}, u32[]{:S(2)}) async-start(bf16[48,4,192]{2,0,1:T(8,128)(2,1)} %copy.99), calls=%async_computation.4 | async-start | bytes 196608 | tf_op jit(solution)/shard_map/all_to_all | solution.py:69
  636.4 122.7 %copy-start = (bf16[48,4,192]{2,0,1:T(8,128)(2,1)S(1)}, bf16[48,4,192]{2,0,1:T(8,128)(2,1)}, u32[]{:S(2)}) copy-start(bf16[48,4,192]{2,0,1:T(8,128)(2,1)} %all_to_all.137) | copy-start | bytes 221188
  711.7 540.2 %all-to-all-start.6 = ((bf16[4,48,192]{2,1,0:T(8,128)(2,1)}), bf16[4,48,192]{2,1,0:T(8,128)(2,1)S(1)}, u32[]{:S(2)}, u32[]{:S(2)}) async-start(bf16[4,48,192]{2,1,0:T(8,128)(2,1)} %copy.131), calls=%async_computation.6 | async-start | bytes 196608 | tf_op jit(solution)/shard_map/all_to_all | solution.py:116
  1234.1 63.5 %copy-start.3 = (f32[192,3]{0,1:T(4,128)S(1)}, f32[192,3]{0,1:T(4,128)}, u32[]{:S(2)}) copy-start(f32[192,3]{0,1:T(4,128)} %param.15) | copy-start | bytes 6916
  1251.9 99.3 %all-to-all-start.7 = ((bf16[4,48,192]{2,1,0:T(8,128)(2,1)}), bf16[4,48,192]{2,1,0:T(8,128)(2,1)S(1)}, u32[]{:S(2)}, u32[]{:S(2)}) async-start(bf16[4,48,192]{2,1,0:T(8,128)(2,1)} %copy.132), calls=%async_computation.7 | async-start | bytes 196608 | tf_op jit(solution)/shard_map/all_to_all | solution.py:117
  1351.2 9.7 all-to-all-start.5
Sparse Core Ops, SparseCore 0:
  19.5 266.6 all-gather.10
  288.0 307.3 all-gather.12
  597.1 306.2 all-gather.6
  905.0 305.7 all-gather.8
where the time goes:
time: 1370 us
  waiting for transfers between devices  644 us (47%)
  blocking collectives  302 us (22%)
  local copies, waits for them, and re-layouts  178 us (13%)
  matrix products  126 us (9%)
  starting transfers between devices  103 us (8%)
  between operations  14 us (1%)
    all_gather x1, waiting for transfers between devices, local(): lax.all_gather(moved[2], 'ctx', axis=0, tiled=True)  266 us
    all_gather x1, waiting for transfers between devices, local(): lax.all_gather(moved[3], 'ctx', axis=0, tiled=True)  232 us
    all_gather x1, waiting for transfers between devices, local(): lax.all_gather(moved[1], 'ctx', axis=0, tiled=True)  143 us
    all_gather x1, blocking collectives, local(): lax.all_gather(logsumexp, 'ctx', axis=0, tiled=True)  135 us
    all_gather x1, blocking collectives, local(): lax.all_gather(deltas, 'ctx', axis=0, tiled=True)  127 us
    another operation x4, local copies, waits for them, and re-layouts, over_blocks(): matrix.reshape((length // block_size, block_size) + matrix.shape[1:])  93 us
    unnamed x18, local copies, waits for them, and re-layouts  72.1 us
    dot_general x12, matrix products, attend(): jnp.einsum('ahd,bhd->hab', query_part, key_part, preferred_element_type=j...  49 us
  transfers between devices with their start and end apart: 8, of which 4 were waited for; matrix products, arithmetic and copies ran while one was open for 22% of the time, Pallas kernels for 0%

commit v1 on v0

--- a/solution.py
+++ b/solution.py
@@ -102,7 +102,9 @@
     grad_query = over_blocks(keys_step, zeros, (key_piece, value_piece))
     pieces = (
         lax.all_gather(moved[0], "ctx", axis=0, tiled=True),
-        lax.all_gather(moved[3], "ctx", axis=0, tiled=True),
+        jnp.concatenate(
+            lax.all_to_all(jnp.stack([moved[3]] * lax.axis_size("ctx")), "ctx", 0, 0), axis=0
+        ),
     )
     query_piece, grad_piece = [split(piece) for piece in pieces]
     grad_key, grad_value = over_blocks(

time: 1370 us -> 1110 us (0.81)
  waiting for transfers between devices: 644 us -> 233 us
  blocking collectives: 302 us -> 439 us
  starting transfers between devices: 103 us -> 124 us
    all_gather x1 -> x0, waiting for transfers between devices: 232 us -> none  [local(): lax.all_gather(moved[3], 'ctx', axis=0, tiled=True)]
    all_gather x1, blocking collectives: 135 us -> 291 us  [local(): lax.all_gather(logsumexp, 'ctx', axis=0, tiled=True)]
    all_gather x1, waiting for transfers between devices: 143 us -> 0.01 us  [local(): lax.all_gather(moved[1], 'ctx', axis=0, tiled=True)]
    all_gather x1, waiting for transfers between devices: 266 us -> 216 us  [local(): lax.all_gather(moved[2], 'ctx', axis=0, tiled=True)]
    all_to_all x2 -> x0, blocking collectives: 19 us -> none  [the longest x1 10.2 us: local(): lax.all_to_all(values, 'head', split_axis=1, concat_axis=0, tiled=True)]
    all_to_all x0 -> x3, starting transfers between devices: none -> 18.8 us  [the longest x1 9.69 us: local(): lax.all_to_all(jnp.stack([moved[3]] * lax.axis_size('ctx')), 'ctx', 0, 0)]
    unnamed x18 -> x20, local copies, waits for them, and re-layouts: 72.1 us -> 61.7 us
  transfers between devices with their start and end apart: 8 -> 10, of which waited for: 4 -> 5; matrix products, arithmetic and copies ran while one was open for 22% -> 26% of each run, Pallas kernels for 0% -> 0%
where the time goes in v1:
time: 1110 us
  blocking collectives  439 us (40%)
  waiting for transfers between devices  233 us (21%)
  local copies, waits for them, and re-layouts  171 us (15%)
  matrix products  126 us (11%)
  starting transfers between devices  124 us (11%)
  between operations  14 us (1%)
    all_gather x1, blocking collectives, local(): lax.all_gather(logsumexp, 'ctx', axis=0, tiled=True)  291 us
    all_gather x1, waiting for transfers between devices, local(): lax.all_gather(moved[2], 'ctx', axis=0, tiled=True)  216 us
    all_gather x1, blocking collectives, local(): lax.all_gather(deltas, 'ctx', axis=0, tiled=True)  128 us
    another operation x4, local copies, waits for them, and re-layouts, over_blocks(): matrix.reshape((length // block_size, block_size) + matrix.shape[1:])  83 us
    unnamed x20, local copies, waits for them, and re-layouts  61.7 us
    all_to_all x1, starting transfers between devices, local(): lax.all_to_all(key_low, 'head', split_axis=0, concat_axis=1, tiled=True)  51.4 us
    dot_general x12, matrix products, attend(): jnp.einsum('ahd,bhd->hab', query_part, key_part, preferred_element_type=j...  49.2 us
    all_to_all x1, starting transfers between devices, local(): lax.all_to_all(value_low, 'head', split_axis=0, concat_axis=1, tiled=True)  45.7 us
  transfers between devices with their start and end apart: 10, of which 5 were waited for; matrix products, arithmetic and copies ran while one was open for 26% of the time, Pallas kernels for 0%

profile of v1, /device:TPU:1, one launch (start us, length us, event | category | flops | bytes accessed | tf_op | source)
XLA Modules:
  0.0 1108.0 jit_solution(7921565743183063632)
XLA Ops:
  7.2 1.0 all_to_all.107
  8.3 11.1 %all_to_all.139 = bf16[48,4,192]{2,0,1:T(8,128)(2,1)} all-to-all(bf16[48,4,192]{2,0,1:T(8,128)(2,1)S(1)} %copy.95), channel_id=1, replica_groups=mesh['ctx'=64,'head'=4] {'head'}, dimensions={1} | all-to-all | bytes 147456 | tf_op jit(solution)/shard_map/all_to_all | solution.py:65
  19.5 1.0 all_to_all.103
  20.5 8.9 all_to_all.140
  29.4 1.0 all_to_all.114
  31.1 4.2 all-to-all-start.3
  35.3 1.0 all_to_all.117
  37.0 4.8 all-to-all-done.3
  41.8 3.6 all-to-all-start.4
  45.4 1.0 all_to_all.110
  47.1 3.4 all-to-all-done.4
  50.5 4.9 all-to-all-start.2
  55.5 5.0 all-to-all-done.2
  60.5 3.4 stack.5
  63.9 9.7 all-to-all-start.6
  74.3 291.0 %all-gather = f32[64,192,3]{1,2,0:T(4,128)S(1)} all-gather(f32[1,192,3]{1,2,0:T(4,128)S(1)} %bitcast.130), channel_id=1, replica_groups=mesh['ctx'=64,'head'=4] {'ctx'}, dimensions={0}, use_global_device_ids=true | all-gather | bytes 149760 | tf_op jit(solution)/shard_map/all_gather | solution.py:94
  366.1 127.9 %all-gather.1 = f32[64,192,3]{1,2,0:T(4,128)S(1)} all-gather(f32[1,192,3]{1,2,0:T(4,128)S(1)} %copy.111), channel_id=1, replica_groups=mesh['ctx'=64,'head'=4] {'ctx'}, dimensions={0}, use_global_device_ids=true | all-gather | bytes 149760 | tf_op jit(solution)/shard_map/all_gather | solution.py:95
  494.8 9.0 copy.110
  503.8 13.2 %reshape_reshape_reshape.3 = bf16[6,2048,3,64]{1,0,3,2:T(8,128)(2,1)} reshape(bf16[64,192,192]{1,0,2:T(8,128)(2,1)} %copy.110) | data formatting | bytes 9437184 | tf_op jit(solution)/shard_map/reshape;reshape;reshape | solution.py:18
  517.0 7.5 copy.116
  524.5 23.3 %reshape.88 = bf16[6,2048,3,64]{3,2,1,0:T(4,128)(2,1)} reshape(bf16[12288,192]{1,0:T(8,128)(2,1)} %all-gather.10.cloned.1.call-done) | data formatting | bytes 9437184 | tf_op jit(solution)/shard_map/reshape;reshape | solution.py:18
  547.7 17.8 %copy.113 = bf16[6,2048,3,64]{1,3,2,0:T(8,128)(2,1)} copy(bf16[6,2048,3,64]{3,2,1,0:T(4,128)(2,1)} %reshape.88) | data formatting | bytes 9437184
  565.5 74.5 %while.25 = (s32[]{:T(128)}, f32[192,3,64]{0,2,1:T(8,128)S(1)}, f32[192,3,64]{0,2,1:T(8,128)S(1)}, bf16[6,2048,3,64]{1,3,2,0:T(8,128)(2,1)}, bf16[192,3,64]{0,2,...) while((s32[]{:T(128)}, f32[192,3,64]{0,2,1:T(8,128)S(1)}, ...), condition=%wide.region_4.5_spmd.clone, body=%wide.region_3.4_spmd.clone.sunk | while | flops 613601280 | bytes 18311292 | solution.py:26
  565.5 4.1 fusion.84
  569.8 4.6 fusion.85
  574.3 3.6 fusion.86
  578.0 4.1 fusion.84
  582.2 4.6 fusion.85
  586.8 3.6 fusion.86
  590.4 4.1 fusion.84
  594.6 4.6 fusion.85
  599.2 3.6 fusion.86
  602.8 4.1 fusion.84
  607.0 4.6 fusion.85
  611.6 3.6 fusion.86
  615.2 4.1 fusion.84
  619.4 4.6 fusion.85
  624.0 3.6 fusion.86
  627.6 4.1 fusion.84
  631.8 4.6 fusion.85
  636.4 3.6 fusion.86
  640.2 0.8 copy.130
  641.0 51.4 %all-to-all-start.7 = ((bf16[4,48,192]{2,1,0:T(8,128)(2,1)}), bf16[4,48,192]{2,1,0:T(8,128)(2,1)S(1)}, u32[]{:S(2)}, u32[]{:S(2)}) async-start(bf16[4,48,192]{2,1,0:T(8,128)(2,1)} %copy.130), calls=%async_computation.7 | async-start | bytes 196608 | tf_op jit(solution)/shard_map/all_to_all | solution.py:118
  693.9 23.3 %reshape.85 = bf16[6,2048,3,64]{3,2,1,0:T(4,128)(2,1)} reshape(bf16[12288,192]{1,0:T(8,128)(2,1)} %all-gather.6.cloned.1.call-done) | data formatting | bytes 9437184 | tf_op jit(solution)/shard_map/reshape;reshape | solution.py:18
  717.2 17.8 %copy.100 = bf16[6,2048,3,64]{1,3,2,0:T(8,128)(2,1)} copy(bf16[6,2048,3,64]{3,2,1,0:T(4,128)(2,1)} %reshape.85) | data formatting | bytes 9437184
  735.0 215.6 %all-gather.8.cloned.1.call-done = bf16[12288,192]{1,0:T(8,128)(2,1)} async-done(((bf16[192,192]{1,0:T(8,128)(2,1)}), bf16[12288,192]{1,0:T(8,128)(2,1)}) %all-gather.8.cloned.1.call-update) | async-done | bytes 4718608 | tf_op jit(solution)/shard_map/all_gather | solution.py:99
  950.6 23.3 %reshape.86 = bf16[6,2048,3,64]{3,2,1,0:T(4,128)(2,1)} reshape(bf16[12288,192]{1,0:T(8,128)(2,1)} %all-gather.8.cloned.1.call-done) | data formatting | bytes 9437184 | tf_op jit(solution)/shard_map/reshape;reshape | solution.py:18
  973.8 17.8 %copy.102 = bf16[6,2048,3,64]{1,3,2,0:T(8,128)(2,1)} copy(bf16[6,2048,3,64]{3,2,1,0:T(4,128)(2,1)} %reshape.86) | data formatting | bytes 9437184
  991.6 45.7 %all-to-all-start.8 = ((bf16[4,48,192]{2,1,0:T(8,128)(2,1)}), bf16[4,48,192]{2,1,0:T(8,128)(2,1)S(1)}, u32[]{:S(2)}, u32[]{:S(2)}) async-start(bf16[4,48,192]{2,1,0:T(8,128)(2,1)} %copy.131), calls=%async_computation.8 | async-start | bytes 196608 | tf_op jit(solution)/shard_map/all_to_all | solution.py:119
  1037.3 52.7 %while.24 = (s32[]{:T(128)}, f32[192,3,64]{0,2,1:T(8,128)S(1)}, bf16[6,2048,3,64]{1,3,2,0:T(8,128)(2,1)}, bf16[192,3,64]{0,2,1:T(8,128)(2,1)S(1)}, f32[192,3]{0,...) while((s32[]{:T(128)}, f32[192,3,64]{0,2,1:T(8,128)S(1)}, ...), condition=%wide.region_2.3_spmd.clone, body=%wide.region_1.2_spmd.clone.sunk | while | flops 458993664 | bytes 12245103 | solution.py:26
  1037.3 4.1 fusion.75
  1041.4 4.7 fusion.76
  1046.1 4.1 fusion.75
  1050.2 4.7 fusion.76
  1054.9 4.1 fusion.75
  1059.0 4.7 fusion.76
  1063.7 4.1 fusion.75
  1067.8 4.7 fusion.76
  1072.5 4.1 fusion.75
  1076.6 4.7 fusion.76
  1081.2 4.1 fusion.75
  1085.3 4.7 fusion.76
  1091.0 4.8 all-to-all-start.5
  1097.4 3.2 all-to-all-done.5
  (79 shorter events, 9.8 us)
Async XLA Ops:
  7.2 517.3 %all-gather.10.cloned.1.call-start = ((), (), s32[]{:S(2)}) async-start(), calls=%async_computation.11 | async-start | bytes 6389760 | tf_op jit(solution)/shard_map/all_gather | solution.py:104
  19.4 674.5 %all-gather.6.cloned.1.call-start = ((), (), s32[]{:S(2)}) async-start(), calls=%async_computation.9 | async-start | bytes 6389760 | tf_op jit(solution)/shard_map/all_gather | solution.py:98
  31.1 10.7 all-to-all-start.3
  41.8 8.7 all-to-all-start.4
  50.5 10.0 all-to-all-start.2
  60.5 3.4 copy-start.2
  63.9 10.5 copy-start.4
  63.9 430.4 %copy-start.1 = (bf16[48,4,192]{2,0,1:T(8,128)(2,1)S(1)}, bf16[48,4,192]{2,0,1:T(8,128)(2,1)}, u32[]{:S(2)}) copy-start(bf16[48,4,192]{2,0,1:T(8,128)(2,1)} %all_to_all.140) | copy-start | bytes 221188
  63.9 430.9 %all-to-all-start.6 = ((bf16[64,192,192]{1,2,0:T(8,128)(2,1)}), bf16[64,192,192]{1,2,0:T(8,128)(2,1)}, u32[]{:S(2)}, u32[]{:S(2)}) async-start(bf16[64,192,192]{1,2,0:T(8,128)(2,1)} %stack.5), calls=%async_computation.6 | async-start | bytes 12582912 | tf_op jit(solution)/shard_map/all_to_all | solution.py:106
  73.6 420.9 %copy-start.3 = (bf16[48,4,192]{2,0,1:T(8,128)(2,1)S(1)}, bf16[48,4,192]{2,0,1:T(8,128)(2,1)}, u32[]{:S(2)}) copy-start(bf16[48,4,192]{2,0,1:T(8,128)(2,1)} %copy-done.2) | copy-start | bytes 221188
  73.6 877.0 %all-gather.8.cloned.1.call-start = ((), (), s32[]{:S(2)}) async-start(), calls=%async_computation.10 | async-start | bytes 6389760 | tf_op jit(solution)/shard_map/all_gather | solution.py:99
  565.5 127.1 %copy-start = (bf16[48,4,192]{2,0,1:T(8,128)(2,1)S(1)}, bf16[48,4,192]{2,0,1:T(8,128)(2,1)}, u32[]{:S(2)}) copy-start(bf16[48,4,192]{2,0,1:T(8,128)(2,1)} %all_to_all.139) | copy-start | bytes 221188
  641.0 350.6 %all-to-all-start.7 = ((bf16[4,48,192]{2,1,0:T(8,128)(2,1)}), bf16[4,48,192]{2,1,0:T(8,128)(2,1)S(1)}, u32[]{:S(2)}, u32[]{:S(2)}) async-start(bf16[4,48,192]{2,1,0:T(8,128)(2,1)} %copy.130), calls=%async_computation.7 | async-start | bytes 196608 | tf_op jit(solution)/shard_map/all_to_all | solution.py:118
  991.6 99.4 %all-to-all-start.8 = ((bf16[4,48,192]{2,1,0:T(8,128)(2,1)}), bf16[4,48,192]{2,1,0:T(8,128)(2,1)S(1)}, u32[]{:S(2)}, u32[]{:S(2)}) async-start(bf16[4,48,192]{2,1,0:T(8,128)(2,1)} %copy.131), calls=%async_computation.8 | async-start | bytes 196608 | tf_op jit(solution)/shard_map/all_to_all | solution.py:119
  1091.0 9.7 all-to-all-start.5
Sparse Core Ops, SparseCore 0:
  19.5 319.1 all-gather.9
  340.5 302.3 all-gather.5
  644.6 305.8 all-gather.7
